TPU v7x, 256 devices: a whole 4x4x8 slice. The times are simulated.
256 devices in a mesh: expert: 16 (over y, x), hidden: 16 (over z, core).
Axes of the slice: x: 4, y: 4, z: 8, core: 2. Of those that a mesh axis runs over, the one named last changes fastest.
Arguments:
- layer_input: bfloat16 [4096, 4096], P('expert', 'hidden'), may hold values from -6 to 6
- output_grad: bfloat16 [4096, 4096], P('expert', 'hidden'), may hold values from -1.5 to 1.5
- latent_saved: bfloat16 [4096, 1024], P('expert'), may hold values from -6 to 6
- combined_saved: bfloat16 [4096, 1024], P('expert'), may hold values from -6 to 6
- expert_ids: int32 [4096, 22], P('expert'), may hold values from 0 to 511, as said below
- gate_values: bfloat16 [4096, 22], P('expert'), may hold values from 0.099609375 to 1.5
- down_proj: bfloat16 [1024, 4096], P(None, 'hidden'), may hold values from -0.09375 to 0.09375
- up_proj: bfloat16 [1024, 4096], P(None, 'hidden'), may hold values from -0.1875 to 0.1875
- expert_in: bfloat16 [16, 1024, 2688], P('expert', None, 'hidden'), may hold values from -0.1875 to 0.1875
- expert_out: bfloat16 [16, 2688, 1024], P('expert', 'hidden'), may hold values from -0.125 to 0.125
Outputs:
- input_grad: bfloat16 [4096, 4096], P('expert', 'hidden')
- down_grad: float32 [1024, 4096], P('expert', 'hidden')
- up_grad: float32 [1024, 4096], P('expert', 'hidden')
- gate_grad: float32 [4096, 22], P('expert')
- expert_in_grad: float32 [16, 1024, 2688], P('expert', None, 'hidden')
- expert_out_grad: float32 [16, 2688, 1024], P('expert', 'hidden')
Inputs may be any that keep to these rules, and one draw needn't show every extreme that they name: `expert_ids`: each row names 22 different experts. In each aligned block of 256 rows (the rows of one index of the expert axis) each expert below 16 is named by at most 24 rows; some expert below 16 is named by exactly 24 rows in every block.
All inputs are finite; a program needn't handle non-finite values.
Results may differ from a plain program's by a relative error of at most 0.0065.
Values may be sent and summed in bfloat16 or wider, within the bound.
No kernel may reach another device: no remote copies, remote signals or barrier semaphores. Data moves between devices by JAX's collectives and lax.ppermute only.
A program may use at most 64 MiB of HBM per device.

v0:
```python
import jax
import jax.numpy as jnp
from jax import lax
from jax.sharding import PartitionSpec as P


def slot_layout(table, groups, local_count):
    tokens_here = table.shape[0]
    return table.T.reshape(groups, local_count, tokens_here).transpose(1, 0, 2)[:, :, None, :]


def on_device(
    layer_input,
    output_grad,
    latent_saved,
    combined_saved,
    expert_ids,
    gate_values,
    down_proj,
    up_proj,
    expert_in,
    expert_out,
):
    groups = lax.axis_size("expert")
    tokens_here = layer_input.shape[0]
    latent_width = latent_saved.shape[1]
    local_count = expert_in.shape[0]
    capacity = tokens_here * 3 // 32
    live_count = local_count * groups
    slot_total = local_count * groups * capacity
    partial_cot = jnp.einsum("td,ld->tl", output_grad, up_proj, preferred_element_type=jnp.float32)
    member = expert_ids[:, :, None] == jnp.arange(live_count, dtype=jnp.int32)[None, None, :]
    per_token = jnp.sum(member.astype(jnp.int32), axis=1)
    before = jnp.cumsum(per_token, axis=0) - per_token
    gate_token = jnp.sum(
        jnp.where(member, gate_values.astype(jnp.float32)[:, :, None], 0.0), axis=1
    )
    rank_iota = jnp.arange(capacity, dtype=jnp.int32)[None, None, :, None]
    hit_slot = (slot_layout(per_token, groups, local_count) == 1) & (
        slot_layout(before, groups, local_count) == rank_iota
    )
    gate_slot = jnp.sum(
        jnp.where(hit_slot, slot_layout(gate_token, groups, local_count), 0.0), axis=3
    )
    gate_send = gate_slot.astype(jnp.bfloat16)
    dispatch_bf = hit_slot.astype(jnp.bfloat16).reshape(slot_total, tokens_here)
    cot_full = lax.psum(partial_cot, "hidden")
    cot_rows = jnp.dot(
        dispatch_bf, cot_full.astype(jnp.bfloat16), preferred_element_type=jnp.float32
    ).astype(jnp.bfloat16)
    latent_rows = jnp.dot(dispatch_bf, latent_saved, preferred_element_type=jnp.float32).astype(
        jnp.bfloat16
    )
    cot_recv, latent_recv, gate_recv = (
        lax.all_to_all(
            cot_rows.reshape(local_count, groups, capacity, latent_width),
            "expert",
            split_axis=1,
            concat_axis=1,
            tiled=True,
        ),
        lax.all_to_all(
            latent_rows.reshape(local_count, groups, capacity, latent_width),
            "expert",
            split_axis=1,
            concat_axis=1,
            tiled=True,
        ),
        lax.all_to_all(gate_send, "expert", split_axis=1, concat_axis=1, tiled=True),
    )
    row_count = groups * capacity
    cot_block = cot_recv.reshape(local_count, row_count, latent_width)
    latent_block = latent_recv.reshape(local_count, row_count, latent_width)
    gate_block = gate_recv.reshape(local_count, row_count).astype(jnp.float32)
    pre_act = jnp.einsum(
        "erl,elf->erf", latent_block, expert_in, preferred_element_type=jnp.float32
    )
    relu_out = jnp.maximum(pre_act, 0.0)
    back_proj = jnp.einsum(
        "erl,efl->erf", cot_block, expert_out, preferred_element_type=jnp.float32
    )
    gate_part = jnp.sum(back_proj * relu_out * relu_out, axis=2)
    scaled_act = (gate_block[:, :, None] * relu_out * relu_out).astype(jnp.bfloat16)
    pre_grad = (2.0 * gate_block[:, :, None] * relu_out * back_proj).astype(jnp.bfloat16)
    expert_out_grad = jnp.einsum(
        "erf,erl->efl", scaled_act, cot_block, preferred_element_type=jnp.float32
    )
    expert_in_grad = jnp.einsum(
        "erl,erf->elf", latent_block, pre_grad, preferred_element_type=jnp.float32
    )
    latent_back = jnp.einsum(
        "erf,elf->erl", pre_grad, expert_in, preferred_element_type=jnp.float32
    )
    latent_back = latent_back.reshape(local_count, groups, capacity, latent_width)
    gate_part = gate_part.reshape(local_count, groups, capacity)
    dispatch_full = hit_slot.astype(jnp.float32)
    dispatch_flat = dispatch_full.reshape(slot_total, tokens_here)
    rows_home, gate_home = (
        lax.all_to_all(latent_back, "expert", split_axis=1, concat_axis=1, tiled=True),
        lax.all_to_all(gate_part, "expert", split_axis=1, concat_axis=1, tiled=True),
    )
    token_sums = jnp.dot(
        dispatch_flat.T,
        rows_home.reshape(slot_total, latent_width),
        precision=lax.Precision.HIGHEST,
        preferred_element_type=jnp.float32,
    )
    by_expert = jnp.sum(dispatch_full * gate_home[:, :, :, None], axis=2)
    by_expert = by_expert.transpose(2, 1, 0).reshape(tokens_here, live_count)
    gate_local = jnp.sum(jnp.where(member, by_expert[:, None, :], 0.0), axis=2)
    latent_grad, gate_grad = lax.psum((token_sums, gate_local), "hidden")
    latent_bf = latent_grad.astype(jnp.bfloat16)
    input_grad = jnp.dot(latent_bf, down_proj, preferred_element_type=jnp.float32).astype(
        jnp.bfloat16
    )
    down_term = jnp.einsum("tl,td->ld", latent_bf, layer_input, preferred_element_type=jnp.float32)
    up_term = jnp.einsum(
        "tl,td->ld", combined_saved, output_grad, preferred_element_type=jnp.float32
    )
    down_grad, up_grad = (
        lax.psum_scatter(down_term, "expert", scatter_dimension=0, tiled=True),
        lax.psum_scatter(up_term, "expert", scatter_dimension=0, tiled=True),
    )
    return (input_grad, down_grad, up_grad, gate_grad, expert_in_grad, expert_out_grad)


def solution(mesh):
    return jax.shard_map(
        on_device,
        mesh=mesh,
        in_specs=(
            P("expert", "hidden"),
            P("expert", "hidden"),
            P("expert", None),
            P("expert", None),
            P("expert", None),
            P("expert", None),
            P(None, "hidden"),
            P(None, "hidden"),
            P("expert", None, "hidden"),
            P("expert", "hidden", None),
        ),
        out_specs=(
            P("expert", "hidden"),
            P("expert", "hidden"),
            P("expert", "hidden"),
            P("expert", None),
            P("expert", None, "hidden"),
            P("expert", "hidden", None),
        ),
        check_vma=False,
    )
```

profile of v0, /device:TPU:2, one launch (start us, length us, event | category | flops | bytes accessed | tf_op | source)
XLA Modules:
  0.0 312.9 jit_solution(7600036610667485425)
XLA Ops:
  7.2 0.8 convert_reduce_fusion
  9.0 1.5 fusion.23
  10.5 62.0 %all-reduce.3 = bf16[256,1024]{1,0:T(8,128)(2,1)S(1)} all-reduce(f32[256,1024]{1,0:T(8,128)S(1)} %fusion.23), channel_id=1, replica_groups=mesh['expert'=16,'hidden'=16] {'hidden'}, use_global_device_ids=true, to_apply=%region_5.6 | all-reduce | flops 262144 | bytes 1572864 | tf_op jit(solution)/shard_map/psum | solution.py:47
  72.7 1.3 convolution_convert_fusion
  73.9 7.5 %all-to-all-start.2 = ((bf16[1,16,24,1024]{3,2,0,1:T(8,128)(2,1)}), bf16[1,16,24,1024]{3,2,0,1:T(8,128)(2,1)S(1)}, u32[]{:S(2)}, u32[]{:S(2)}) async-start(bf16[1,16,24,1024]{3,2,0,1:T(8,128)(2,1)} %bitcast.11), calls=%async_computation.2 | async-start | bytes 1572864 | tf_op jit(solution)/shard_map/all_to_all | solution.py:55
  81.4 1.3 convolution_convert_fusion.1
  82.7 8.9 %all-to-all-done.2 = bf16[1,16,24,1024]{3,2,0,1:T(8,128)(2,1)S(1)} async-done(((bf16[1,16,24,1024]{3,2,0,1:T(8,128)(2,1)}), bf16[1,16,24,1024]{3,2,0,1:T(8,128)(2,1)S(1)}, u32[]{:S(2)}, u32[]{:S(2)}) %all-to-all-start.2) | async-done | bytes 786464 | tf_op jit(solution)/shard_map/all_to_all | solution.py:55
  91.6 4.9 %all-to-all-start.1 = ((bf16[1,16,24,1024]{3,2,0,1:T(8,128)(2,1)}), bf16[1,16,24,1024]{3,2,0,1:T(8,128)(2,1)S(1)}, u32[]{:S(2)}, u32[]{:S(2)}) async-start(bf16[1,16,24,1024]{3,2,0,1:T(8,128)(2,1)} %bitcast.7), calls=%async_computation.1 | async-start | bytes 1572864 | tf_op jit(solution)/shard_map/all_to_all | solution.py:62
  96.9 9.9 %all-to-all-done.1 = bf16[1,16,24,1024]{3,2,0,1:T(8,128)(2,1)S(1)} async-done(((bf16[1,16,24,1024]{3,2,0,1:T(8,128)(2,1)}), bf16[1,16,24,1024]{3,2,0,1:T(8,128)(2,1)S(1)}, u32[]{:S(2)}, u32[]{:S(2)}) %all-to-all-start.1) | async-done | bytes 786464 | tf_op jit(solution)/shard_map/all_to_all | solution.py:62
  107.2 0.7 reshape.184
  107.9 4.7 %all-to-all-start.4 = ((f32[1,16,24]{2,0,1:T(1,128)}), f32[1,16,24]{2,0,1:T(1,128)S(1)}, u32[]{:S(2)}, u32[]{:S(2)}) async-start(f32[1,16,24]{2,0,1:T(1,128)} %reshape.184), calls=%async_computation.6 | async-start | bytes 16384 | tf_op jit(solution)/shard_map/all_to_all | solution.py:100
  112.7 6.2 %all-to-all-done.4 = f32[1,16,24]{2,0,1:T(1,128)S(1)} async-done(((f32[1,16,24]{2,0,1:T(1,128)}), f32[1,16,24]{2,0,1:T(1,128)S(1)}, u32[]{:S(2)}, u32[]{:S(2)}) %all-to-all-start.4) | async-done | bytes 1568 | tf_op jit(solution)/shard_map/all_to_all | solution.py:100
  119.4 10.6 %all_to_all.25 = bf16[1,16,24]{2,0,1:T(2,128)(2,1)S(1)} all-to-all(bf16[1,16,24]{2,0,1:T(2,128)(2,1)S(1)} %copy.45), channel_id=1, replica_groups=mesh['expert'=16,'hidden'=16] {'expert'}, dimensions={1} | all-to-all | bytes 1536 | tf_op jit(solution)/shard_map/all_to_all | solution.py:69
  130.3 1.5 convolution_bitcast_fusion
  131.8 5.7 %all-to-all-start.3 = ((f32[1,16,24,1024]{3,2,0,1:T(8,128)}), f32[1,16,24,1024]{3,2,0,1:T(8,128)}, u32[]{:S(2)}, u32[]{:S(2)}) async-start(f32[1,16,24,1024]{3,2,0,1:T(8,128)} %convolution_bitcast_fusion), calls=%async_computation.3 | async-start | bytes 3145728 | tf_op jit(solution)/shard_map/all_to_all | solution.py:99
  137.6 1.3 fusion.24
  139.0 13.1 %all-to-all-done.3 = f32[1,16,24,1024]{3,2,0,1:T(8,128)} async-done(((f32[1,16,24,1024]{3,2,0,1:T(8,128)}), f32[1,16,24,1024]{3,2,0,1:T(8,128)}, u32[]{:S(2)}, u32[]{:S(2)}) %all-to-all-start.3) | async-done | bytes 1572896 | tf_op jit(solution)/shard_map/all_to_all | solution.py:99
  152.1 3.5 %fusion.2 = f32[256,1024]{1,0:T(8,128)} fusion(f32[1,16,24,1024]{3,2,0,1:T(8,128)} %all-to-all-done.3, s32[16,256]{1,0:T(8,128)S(1)} %bitcast_subtract_fusion, pred[16,256]{1,0:T(8,128)(4,1)S(1)} %bitcast_compare_fusion.1), kind=kOutput, calls=%fused_computation.5 | convolution fusion | flops 1208156160 | bytes 2641920 | tf_op jit(solution)/shard_map/dot_general | solution.py:102
  155.7 66.5 %all-reduce.4 = (bf16[256,1024]{1,0:T(8,128)(2,1)S(1)}, f32[256,22]{0,1:T(8,128)}) all-reduce(f32[256,1024]{1,0:T(8,128)} %fusion.2, f32[256,22]{0,1:T(8,128)S(1)} %get-tuple-element.6), channel_id=1, replica_groups=mesh['expert'=16,'hidden'=16] {'hidden'}, use_global_device_ids=true, to_apply=%region_6.7 | all-reduce | flops 267776 | bytes 1617920 | tf_op jit(solution)/shard_map/psum | solution.py:111
  222.1 1.3 fusion.25
  223.5 1.2 convolution_bitcast_fusion.2
  224.7 1.2 convolution_bitcast_fusion.1
  225.9 1.0 convolution_convert_fusion.2
  226.9 79.2 %reduce-scatter.3.cloned.1.call-done = f32[64,256]{1,0:T(8,128)} async-done(((f32[1024,256]{1,0:T(8,128)}), f32[64,256]{1,0:T(8,128)}) %reduce-scatter.3.cloned.1.call-update) | async-done | bytes 65552 | tf_op jit(solution)/shard_map/reduce_scatter | solution.py:121
  (45 shorter events, 2.9 us)
Async XLA Ops:
  7.2 74.3 %copy-start = (bf16[256,1024]{1,0:T(8,128)(2,1)S(1)}, bf16[256,1024]{1,0:T(8,128)(2,1)}, u32[]{:S(2)}) copy-start(bf16[256,1024]{1,0:T(8,128)(2,1)} %param.12) | copy-start | bytes 1572868
  73.9 17.7 %all-to-all-start.2 = ((bf16[1,16,24,1024]{3,2,0,1:T(8,128)(2,1)}), bf16[1,16,24,1024]{3,2,0,1:T(8,128)(2,1)S(1)}, u32[]{:S(2)}, u32[]{:S(2)}) async-start(bf16[1,16,24,1024]{3,2,0,1:T(8,128)(2,1)} %bitcast.11), calls=%async_computation.2 | async-start | bytes 1572864 | tf_op jit(solution)/shard_map/all_to_all | solution.py:55
  81.4 15.1 %copy-start.5 = (bf16[1,168,1024]{2,1,0:T(8,128)(2,1)S(1)}, bf16[1,168,1024]{2,1,0:T(8,128)(2,1)}, u32[]{:S(2)}) copy-start(bf16[1,168,1024]{2,1,0:T(8,128)(2,1)} %param.19) | copy-start | bytes 1032196
  82.7 24.0 %copy-start.1 = (bf16[1,1024,168]{1,2,0:T(8,128)(2,1)S(1)}, bf16[1,1024,168]{1,2,0:T(8,128)(2,1)}, u32[]{:S(2)}) copy-start(bf16[1,1024,168]{1,2,0:T(8,128)(2,1)} %param.18) | copy-start | bytes 1032196
  91.6 15.2 %all-to-all-start.1 = ((bf16[1,16,24,1024]{3,2,0,1:T(8,128)(2,1)}), bf16[1,16,24,1024]{3,2,0,1:T(8,128)(2,1)S(1)}, u32[]{:S(2)}, u32[]{:S(2)}) async-start(bf16[1,16,24,1024]{3,2,0,1:T(8,128)(2,1)} %bitcast.7), calls=%async_computation.1 | async-start | bytes 1572864 | tf_op jit(solution)/shard_map/all_to_all | solution.py:62
  96.5 16.2 %copy-start.8 = (bf16[256,22]{0,1:T(8,128)(2,1)S(1)}, bf16[256,22]{0,1:T(8,128)(2,1)}, u32[]{:S(2)}) copy-start(bf16[256,22]{0,1:T(8,128)(2,1)} %param.15) | copy-start | bytes 33796
  96.5 22.5 %copy-start.7 = (s32[256,22]{0,1:T(8,128)S(1)}, s32[256,22]{0,1:T(8,128)}, u32[]{:S(2)}) copy-start(s32[256,22]{0,1:T(8,128)} %param.14) | copy-start | bytes 67588
  107.9 10.9 %all-to-all-start.4 = ((f32[1,16,24]{2,0,1:T(1,128)}), f32[1,16,24]{2,0,1:T(1,128)S(1)}, u32[]{:S(2)}, u32[]{:S(2)}) async-start(f32[1,16,24]{2,0,1:T(1,128)} %reshape.184), calls=%async_computation.6 | async-start | bytes 16384 | tf_op jit(solution)/shard_map/all_to_all | solution.py:100
  131.8 5.8 %copy-start.2 = (bf16[256,1024]{1,0:T(8,128)(2,1)S(1)}, bf16[256,1024]{1,0:T(8,128)(2,1)}, u32[]{:S(2)}) copy-start(bf16[256,1024]{1,0:T(8,128)(2,1)} %param.13) | copy-start | bytes 1572868
  131.8 5.8 %copy-start.4 = (bf16[256,256]{1,0:T(8,128)(2,1)S(1)}, bf16[256,256]{1,0:T(8,128)(2,1)}, u32[]{:S(2)}) copy-start(bf16[256,256]{1,0:T(8,128)(2,1)} %param.11) | copy-start | bytes 393220
  131.8 20.3 %all-to-all-start.3 = ((f32[1,16,24,1024]{3,2,0,1:T(8,128)}), f32[1,16,24,1024]{3,2,0,1:T(8,128)}, u32[]{:S(2)}, u32[]{:S(2)}) async-start(f32[1,16,24,1024]{3,2,0,1:T(8,128)} %convolution_bitcast_fusion), calls=%async_computation.3 | async-start | bytes 3145728 | tf_op jit(solution)/shard_map/all_to_all | solution.py:99
  137.5 89.4 %reduce-scatter.5.cloned.1.call-start = ((), (), s32[]{:S(2)}) async-start(), calls=%async_computation.8 | async-start | bytes 1114112 | tf_op jit(solution)/shard_map/reduce_scatter | solution.py:122
  138.9 83.2 %copy-start.6 = (bf16[256,256]{1,0:T(8,128)(2,1)S(1)}, bf16[256,256]{1,0:T(8,128)(2,1)}, u32[]{:S(2)}) copy-start(bf16[256,256]{1,0:T(8,128)(2,1)} %param.10) | copy-start | bytes 393220
  138.9 167.1 %reduce-scatter.3.cloned.1.call-start = ((), (), s32[]{:S(2)}) async-start(), calls=%async_computation.7 | async-start | bytes 1114112 | tf_op jit(solution)/shard_map/reduce_scatter | solution.py:121
  223.5 2.4 copy-start.3
Sparse Core Ops, SparseCore 0:
  142.4 81.0 reduce-scatter.4
  227.6 78.4 reduce-scatter.2
where the time goes:
time: 313 us
  blocking collectives  139 us (44%)
  waiting for transfers between devices  117 us (37%)
  starting transfers between devices  22.9 us (7%)
  matrix products  15.9 us (5%)
  between operations  14.3 us (5%)
    reduce_scatter x1, waiting for transfers between devices, on_device(): lax.psum_scatter(down_term, 'expert', scatter_dimension=0, tiled=True)  79.2 us
    psum x1, blocking collectives, on_device(): latent_grad, gate_grad = lax.psum((token_sums, gate_local), 'hidden')  66.5 us
    psum x1, blocking collectives, on_device(): cot_full = lax.psum(partial_cot, 'hidden')  62 us
    all_to_all x1, waiting for transfers between devices, on_device(): lax.all_to_all(latent_back, 'expert', split_axis=1, concat_axis=1, tiled=...  13.1 us
    all_to_all x1, blocking collectives, on_device(): lax.all_to_all(gate_send, 'expert', split_axis=1, concat_axis=1, tiled=True)  10.6 us
    all_to_all x1, waiting for transfers between devices, on_device(): lax.all_to_all(latent_rows.reshape(local_count, groups, capacity, latent_...  9.86 us
    all_to_all x1, waiting for transfers between devices, on_device(): lax.all_to_all(cot_rows.reshape(local_count, groups, capacity, latent_wid...  8.87 us
    all_to_all x1, starting transfers between devices, on_device(): lax.all_to_all(cot_rows.reshape(local_count, groups, capacity, latent_wid...  7.48 us
  transfers between devices with their start and end apart: 6, of which 5 were waited for; matrix products, arithmetic and copies ran while one was open for 4% of the time, Pallas kernels for 0%

commit v1 on v0

--- a/solution.py
+++ b/solution.py
@@ -44,7 +44,7 @@
     )
     gate_send = gate_slot.astype(jnp.bfloat16)
     dispatch_bf = hit_slot.astype(jnp.bfloat16).reshape(slot_total, tokens_here)
-    cot_full = lax.psum(partial_cot, "hidden")
+    cot_full = jnp.sum(lax.all_gather(partial_cot, "hidden"), axis=0)
     cot_rows = jnp.dot(
         dispatch_bf, cot_full.astype(jnp.bfloat16), preferred_element_type=jnp.float32
     ).astype(jnp.bfloat16)

time: 313 us -> 359 us (1.15)
  waiting for transfers between devices: 117 us -> 224 us
  blocking collectives: 139 us -> 68.5 us
  other arithmetic: 2.22 us -> 9.14 us
    all_gather x0 -> x1, waiting for transfers between devices: none -> 97.2 us  [on_device(): cot_full = jnp.sum(lax.all_gather(partial_cot, 'hidden'), axis=0)]
    psum x1 -> x0, blocking collectives: 62 us -> none  [on_device(): cot_full = lax.psum(partial_cot, 'hidden')]
    psum x1, blocking collectives: 66.5 us -> 57.9 us  [on_device(): latent_grad, gate_grad = lax.psum((token_sums, gate_local), 'hidden')]
    reduce_sum x0 -> x1, other arithmetic: none -> 7.72 us  [on_device(): cot_full = jnp.sum(lax.all_gather(partial_cot, 'hidden'), axis=0)]
    all_to_all x1, waiting for transfers between devices: 13.1 us -> 17.5 us  [on_device(): lax.all_to_all(latent_back, 'expert', split_axis=1, concat_axis=1, tiled=...]
  transfers between devices with their start and end apart: 6 -> 7, of which waited for: 5 -> 6; matrix products, arithmetic and copies ran while one was open for 4% -> 3% of each run, Pallas kernels for 0% -> 0%
where the time goes in v1:
time: 359 us; the launch traced here: 358 us
  waiting for transfers between devices  224 us (62%)
  blocking collectives  68.5 us (19%)
  starting transfers between devices  22.6 us (6%)
  matrix products  17 us (5%)
  between operations  15.7 us (4%)
  other arithmetic  9.14 us (3%)
    all_gather x1, waiting for transfers between devices, on_device(): cot_full = jnp.sum(lax.all_gather(partial_cot, 'hidden'), axis=0)  97.2 us
    reduce_scatter x1, waiting for transfers between devices, on_device(): lax.psum_scatter(down_term, 'expert', scatter_dimension=0, tiled=True)  79.1 us
    psum x1, blocking collectives, on_device(): latent_grad, gate_grad = lax.psum((token_sums, gate_local), 'hidden')  57.9 us
    all_to_all x1, waiting for transfers between devices, on_device(): lax.all_to_all(latent_back, 'expert', split_axis=1, concat_axis=1, tiled=...  17.5 us
    all_to_all x1, waiting for transfers between devices, on_device(): lax.all_to_all(cot_rows.reshape(local_count, groups, capacity, latent_wid...  12.2 us
    all_to_all x1, waiting for transfers between devices, on_device(): lax.all_to_all(latent_rows.reshape(local_count, groups, capacity, latent_...  12 us
    all_to_all x1, blocking collectives, on_device(): lax.all_to_all(gate_send, 'expert', split_axis=1, concat_axis=1, tiled=True)  10.6 us
    reduce_sum x1, other arithmetic, on_device(): cot_full = jnp.sum(lax.all_gather(partial_cot, 'hidden'), axis=0)  7.72 us
  transfers between devices with their start and end apart: 7, of which 6 were waited for; matrix products, arithmetic and copies ran while one was open for 3% of the time, Pallas kernels for 0%

profile of v1, /device:TPU:2, one launch (start us, length us, event | category | flops | bytes accessed | tf_op | source)
XLA Modules:
  0.0 358.4 jit_solution(8465886604232787866)
XLA Ops:
  8.1 2.5 fusion.23
  11.8 97.2 %all-gather.3.cloned.1.call-done = f32[4096,1024]{1,0:T(8,128)} async-done(((f32[256,1024]{1,0:T(8,128)}), f32[4096,1024]{1,0:T(8,128)}) %all-gather.3.cloned.1.call-update) | async-done | bytes 16777232 | tf_op jit(solution)/shard_map/all_gather | solution.py:47
  109.0 7.7 %reduce_sum.68 = bf16[256,1024]{1,0:T(8,128)(2,1)S(1)} reduce(f32[16,256,1024]{2,1,0:T(8,128)} %bitcast.86, f32[]{:T(128)} %constant.3.clone.1), dimensions={0}, to_apply=%region_5.6 | reduce | flops 3932160 | bytes 17301508 | tf_op jit(solution)/shard_map/reduce_sum | solution.py:47
  116.8 1.3 convolution_convert_fusion
  118.0 7.3 %all-to-all-start.2 = ((bf16[1,16,24,1024]{3,2,0,1:T(8,128)(2,1)}), bf16[1,16,24,1024]{3,2,0,1:T(8,128)(2,1)S(1)}, u32[]{:S(2)}, u32[]{:S(2)}) async-start(bf16[1,16,24,1024]{3,2,0,1:T(8,128)(2,1)} %bitcast.12), calls=%async_computation.2 | async-start | bytes 1572864 | tf_op jit(solution)/shard_map/all_to_all | solution.py:55
  125.3 1.3 convolution_convert_fusion.1
  126.6 12.2 %all-to-all-done.2 = bf16[1,16,24,1024]{3,2,0,1:T(8,128)(2,1)S(1)} async-done(((bf16[1,16,24,1024]{3,2,0,1:T(8,128)(2,1)}), bf16[1,16,24,1024]{3,2,0,1:T(8,128)(2,1)S(1)}, u32[]{:S(2)}, u32[]{:S(2)}) %all-to-all-start.2) | async-done | bytes 786464 | tf_op jit(solution)/shard_map/all_to_all | solution.py:55
  138.7 4.8 %all-to-all-start.1 = ((bf16[1,16,24,1024]{3,2,0,1:T(8,128)(2,1)}), bf16[1,16,24,1024]{3,2,0,1:T(8,128)(2,1)S(1)}, u32[]{:S(2)}, u32[]{:S(2)}) async-start(bf16[1,16,24,1024]{3,2,0,1:T(8,128)(2,1)} %bitcast.7), calls=%async_computation.1 | async-start | bytes 1572864 | tf_op jit(solution)/shard_map/all_to_all | solution.py:62
  144.0 12.0 %all-to-all-done.1 = bf16[1,16,24,1024]{3,2,0,1:T(8,128)(2,1)S(1)} async-done(((bf16[1,16,24,1024]{3,2,0,1:T(8,128)(2,1)}), bf16[1,16,24,1024]{3,2,0,1:T(8,128)(2,1)S(1)}, u32[]{:S(2)}, u32[]{:S(2)}) %all-to-all-start.1) | async-done | bytes 786464 | tf_op jit(solution)/shard_map/all_to_all | solution.py:62
  156.5 0.7 reshape.184
  157.2 4.7 %all-to-all-start.4 = ((f32[1,16,24]{2,0,1:T(1,128)}), f32[1,16,24]{2,0,1:T(1,128)S(1)}, u32[]{:S(2)}, u32[]{:S(2)}) async-start(f32[1,16,24]{2,0,1:T(1,128)} %reshape.184), calls=%async_computation.6 | async-start | bytes 16384 | tf_op jit(solution)/shard_map/all_to_all | solution.py:100
  161.9 6.2 %all-to-all-done.4 = f32[1,16,24]{2,0,1:T(1,128)S(1)} async-done(((f32[1,16,24]{2,0,1:T(1,128)}), f32[1,16,24]{2,0,1:T(1,128)S(1)}, u32[]{:S(2)}, u32[]{:S(2)}) %all-to-all-start.4) | async-done | bytes 1568 | tf_op jit(solution)/shard_map/all_to_all | solution.py:100
  168.5 10.6 %all_to_all.25 = bf16[1,16,24]{2,0,1:T(2,128)(2,1)S(1)} all-to-all(bf16[1,16,24]{2,0,1:T(2,128)(2,1)S(1)} %copy.45), channel_id=1, replica_groups=mesh['expert'=16,'hidden'=16] {'expert'}, dimensions={1} | all-to-all | bytes 1536 | tf_op jit(solution)/shard_map/all_to_all | solution.py:69
  179.5 1.5 convolution_bitcast_fusion
  181.0 5.7 %all-to-all-start.3 = ((f32[1,16,24,1024]{3,2,0,1:T(8,128)}), f32[1,16,24,1024]{3,2,0,1:T(8,128)}, u32[]{:S(2)}, u32[]{:S(2)}) async-start(f32[1,16,24,1024]{3,2,0,1:T(8,128)} %convolution_bitcast_fusion), calls=%async_computation.3 | async-start | bytes 3145728 | tf_op jit(solution)/shard_map/all_to_all | solution.py:99
  186.8 1.3 fusion.24
  188.2 17.5 %all-to-all-done.3 = f32[1,16,24,1024]{3,2,0,1:T(8,128)} async-done(((f32[1,16,24,1024]{3,2,0,1:T(8,128)}), f32[1,16,24,1024]{3,2,0,1:T(8,128)}, u32[]{:S(2)}, u32[]{:S(2)}) %all-to-all-start.3) | async-done | bytes 1572896 | tf_op jit(solution)/shard_map/all_to_all | solution.py:99
  205.7 3.5 fusion.2
  209.2 57.9 %all-reduce.2 = (bf16[256,1024]{1,0:T(8,128)(2,1)S(1)}, f32[256,22]{0,1:T(8,128)}) all-reduce(f32[256,1024]{1,0:T(8,128)} %fusion.2, f32[256,22]{0,1:T(8,128)S(1)} %get-tuple-element.6), channel_id=1, replica_groups=mesh['expert'=16,'hidden'=16] {'hidden'}, use_global_device_ids=true, to_apply=%region_6.7 | all-reduce | flops 267776 | bytes 1617920 | tf_op jit(solution)/shard_map/psum | solution.py:111
  267.1 1.3 fusion.25
  268.5 1.2 convolution_bitcast_fusion.2
  269.7 1.2 convolution_bitcast_fusion.1
  270.9 1.0 convolution_convert_fusion.2
  271.8 79.1 %reduce-scatter.3.cloned.1.call-done = f32[64,256]{1,0:T(8,128)} async-done(((f32[1024,256]{1,0:T(8,128)}), f32[64,256]{1,0:T(8,128)}) %reduce-scatter.3.cloned.1.call-update) | async-done | bytes 65552 | tf_op jit(solution)/shard_map/reduce_scatter | solution.py:121
  (48 shorter events, 3.0 us)
Async XLA Ops:
  8.0 117.3 %copy-start = (bf16[256,1024]{1,0:T(8,128)(2,1)S(1)}, bf16[256,1024]{1,0:T(8,128)(2,1)}, u32[]{:S(2)}) copy-start(bf16[256,1024]{1,0:T(8,128)(2,1)} %param.12) | copy-start | bytes 1572868
  8.0 2.6 copy-start.7
  8.0 101.0 %all-gather.3.cloned.1.call-start = ((), (), s32[]{:S(2)}) async-start(), calls=%async_computation.9 | async-start | bytes 17825792 | tf_op jit(solution)/shard_map/all_gather | solution.py:47
  118.0 20.7 %all-to-all-start.2 = ((bf16[1,16,24,1024]{3,2,0,1:T(8,128)(2,1)}), bf16[1,16,24,1024]{3,2,0,1:T(8,128)(2,1)S(1)}, u32[]{:S(2)}, u32[]{:S(2)}) async-start(bf16[1,16,24,1024]{3,2,0,1:T(8,128)(2,1)} %bitcast.12), calls=%async_computation.2 | async-start | bytes 1572864 | tf_op jit(solution)/shard_map/all_to_all | solution.py:55
  125.3 18.3 %copy-start.5 = (bf16[1,168,1024]{2,1,0:T(8,128)(2,1)S(1)}, bf16[1,168,1024]{2,1,0:T(8,128)(2,1)}, u32[]{:S(2)}) copy-start(bf16[1,168,1024]{2,1,0:T(8,128)(2,1)} %param.19) | copy-start | bytes 1032196
  126.6 29.4 %copy-start.1 = (bf16[1,1024,168]{1,2,0:T(8,128)(2,1)S(1)}, bf16[1,1024,168]{1,2,0:T(8,128)(2,1)}, u32[]{:S(2)}) copy-start(bf16[1,1024,168]{1,2,0:T(8,128)(2,1)} %param.18) | copy-start | bytes 1032196
  138.7 17.3 %all-to-all-start.1 = ((bf16[1,16,24,1024]{3,2,0,1:T(8,128)(2,1)}), bf16[1,16,24,1024]{3,2,0,1:T(8,128)(2,1)S(1)}, u32[]{:S(2)}, u32[]{:S(2)}) async-start(bf16[1,16,24,1024]{3,2,0,1:T(8,128)(2,1)} %bitcast.7), calls=%async_computation.1 | async-start | bytes 1572864 | tf_op jit(solution)/shard_map/all_to_all | solution.py:62
  143.5 18.3 %copy-start.8 = (bf16[256,22]{0,1:T(8,128)(2,1)S(1)}, bf16[256,22]{0,1:T(8,128)(2,1)}, u32[]{:S(2)}) copy-start(bf16[256,22]{0,1:T(8,128)(2,1)} %param.15) | copy-start | bytes 33796
  157.2 10.9 %all-to-all-start.4 = ((f32[1,16,24]{2,0,1:T(1,128)}), f32[1,16,24]{2,0,1:T(1,128)S(1)}, u32[]{:S(2)}, u32[]{:S(2)}) async-start(f32[1,16,24]{2,0,1:T(1,128)} %reshape.184), calls=%async_computation.6 | async-start | bytes 16384 | tf_op jit(solution)/shard_map/all_to_all | solution.py:100
  181.0 5.8 %copy-start.2 = (bf16[256,1024]{1,0:T(8,128)(2,1)S(1)}, bf16[256,1024]{1,0:T(8,128)(2,1)}, u32[]{:S(2)}) copy-start(bf16[256,1024]{1,0:T(8,128)(2,1)} %param.13) | copy-start | bytes 1572868
  181.0 5.8 %copy-start.4 = (bf16[256,256]{1,0:T(8,128)(2,1)S(1)}, bf16[256,256]{1,0:T(8,128)(2,1)}, u32[]{:S(2)}) copy-start(bf16[256,256]{1,0:T(8,128)(2,1)} %param.11) | copy-start | bytes 393220
  181.0 24.7 %all-to-all-start.3 = ((f32[1,16,24,1024]{3,2,0,1:T(8,128)}), f32[1,16,24,1024]{3,2,0,1:T(8,128)}, u32[]{:S(2)}, u32[]{:S(2)}) async-start(f32[1,16,24,1024]{3,2,0,1:T(8,128)} %convolution_bitcast_fusion), calls=%async_computation.3 | async-start | bytes 3145728 | tf_op jit(solution)/shard_map/all_to_all | solution.py:99
  186.7 85.1 %reduce-scatter.5.cloned.1.call-start = ((), (), s32[]{:S(2)}) async-start(), calls=%async_computation.8 | async-start | bytes 1114112 | tf_op jit(solution)/shard_map/reduce_scatter | solution.py:122
  188.1 79.0 %copy-start.6 = (bf16[256,256]{1,0:T(8,128)(2,1)S(1)}, bf16[256,256]{1,0:T(8,128)(2,1)}, u32[]{:S(2)}) copy-start(bf16[256,256]{1,0:T(8,128)(2,1)} %param.10) | copy-start | bytes 393220
  188.1 162.8 %reduce-scatter.3.cloned.1.call-start = ((), (), s32[]{:S(2)}) async-start(), calls=%async_computation.7 | async-start | bytes 1114112 | tf_op jit(solution)/shard_map/reduce_scatter | solution.py:121
  268.5 2.4 copy-start.3
Sparse Core Ops, SparseCore 0:
  10.7 98.2 all-gather.2
Sparse Core Ops, SparseCore 1:
  191.2 77.2 reduce-scatter.4
  272.5 78.4 reduce-scatter.2
